TPU v7x, 32 devices: a whole 2x2x4 slice. The times are simulated.
32 devices in a mesh: dp: 16 (over z, y, core), mp: 2 (over x).
Axes of the slice: x: 2, y: 2, z: 4, core: 2. Of those that a mesh axis runs over, the one named last changes fastest.
Arguments:
- hidden_in: bfloat16 [8192, 4096], P('dp'), may hold values from -1.5 to 1.5
- w_query: bfloat16 [4096, 4096], P('dp', 'mp'), may hold values from -1 to 1
- w_key: bfloat16 [4096, 1024], P('dp', 'mp'), may hold values from -24 to 24
- w_value: bfloat16 [4096, 1024], P('dp', 'mp'), may hold values from -1 to 1
- w_out: bfloat16 [4096, 4096], P('dp', 'mp'), may hold values from -1 to 1
- value_weight: float32 [4096], P('mp'), may hold values from -0.09375 to 0.09375
- rewards: float32 [8192], P('dp'), may hold values from -0.6 to 0.6
- old_values: float32 [8192], P('dp'), may hold values from -6 to 6
- lengths: int32 [64], replicated, may hold values from 1 to 2048, 8192 in all
- terminal: int32 [64], replicated, may hold values 0 or 1
Outputs:
- value: float32 [8192], P('dp')
- advantage: float32 [8192], P('dp')
- value_loss: float32 [], replicated
All inputs are finite; a program needn't handle non-finite values.
Results may differ from a plain program's by a relative error of at most 0.012.
The roundings to bfloat16 on the way count: a program that leaves them out, or rounds other values in their place, can miss the bound.
Values may be sent and summed in bfloat16 or wider, within the bound.
No kernel may reach another device: no remote copies, remote signals or barrier semaphores. Data moves between devices by JAX's collectives and lax.ppermute only.
A program may use at most 128 MiB of HBM per device.

v0:
```python
import jax
import jax.numpy as jnp
from jax import lax
from jax.sharding import PartitionSpec as P

HEAD = 128
discount = 0.999
trace_decay = 0.997
clip_range = 0.2
epsilon = 1e-05
rope_base = 500000.0


def from_behind(array, axis, by):
    size = lax.axis_size(axis)
    pairs = [(i, i + by) for i in range(size) if 0 <= i + by < size]
    return lax.ppermute(array, axis, pairs)


def carried_in(part, axis, combine, identity):
    count = lax.axis_size(axis)
    place = lax.axis_index(axis)
    ahead = count - 1 - place
    gathered = jax.tree.map(lambda a: lax.all_gather(a, axis), part)
    state = jax.tree.map(lambda a, e: jnp.zeros_like(a) + jnp.asarray(e, a.dtype), part, identity)

    def one(hop, state):
        source = count - 1 - hop
        return combine(
            state, jax.tree.map(lambda a: lax.dynamic_index_in_dim(a, source, 0, False), gathered)
        )

    return lax.fori_loop(0, ahead, one, state)


def rotate(states, positions):
    half = HEAD // 2
    freq = rope_base ** (-jnp.arange(half, dtype=jnp.float32) * 2.0 / HEAD)
    angles = positions[:, None] * freq[None, :]
    cosine = jnp.cos(angles)[:, None, :]
    sine = jnp.sin(angles)[:, None, :]
    first = states[..., :half]
    second = states[..., half:]
    return jnp.concatenate([first * cosine - second * sine, second * cosine + first * sine], -1)


def body(
    hidden_in, w_query, w_key, w_value, w_out, value_weight, rewards, old_values, lengths, terminal
):
    rows = hidden_in.shape[0]
    width = hidden_in.shape[1]
    states = hidden_in.astype(jnp.float32)
    normed = (states * lax.rsqrt(jnp.mean(states * states, 1, keepdims=True) + epsilon)).astype(
        jnp.bfloat16
    )
    pieces = (
        lax.all_gather(w_query, "dp", axis=0, tiled=True),
        lax.all_gather(w_key, "dp", axis=0, tiled=True),
        lax.all_gather(w_value, "dp", axis=0, tiled=True),
        lax.all_gather(w_out, "dp", axis=0, tiled=True),
    )
    add_pieces = pieces[:3]
    summed = tuple(
        (jnp.dot(normed, piece, preferred_element_type=jnp.float32) for piece in add_pieces)
    )
    stored = pieces[3]
    query_sum, key_sum, value_sum, whole_out = summed + (stored,)
    position_ids = lax.axis_index("dp") * rows + jnp.arange(rows, dtype=jnp.int32)
    positions = position_ids.astype(jnp.float32)
    local_heads = w_query.shape[1] // HEAD
    local_kv = w_key.shape[1] // HEAD
    group = local_heads // local_kv
    query = rotate(query_sum.reshape(rows, local_heads, HEAD), positions).astype(jnp.bfloat16)
    key = rotate(key_sum.reshape(rows, local_kv, HEAD), positions).astype(jnp.bfloat16)
    values_proj = value_sum.astype(jnp.bfloat16).reshape(rows, local_kv, HEAD)
    ends = jnp.cumsum(lengths)
    matches = ends[None, :] - 1 == position_ids[:, None]
    finished = jnp.any(matches, 1).astype(jnp.float32)
    stopped = jnp.sum(jnp.where(matches, terminal[None, :], 0), 1).astype(jnp.float32)
    episode = jnp.sum((ends[None, :] <= position_ids[:, None]).astype(jnp.int32), 1)
    order = jnp.arange(rows, dtype=jnp.int32)
    same_episode = episode[None, :] == episode[:, None]
    allowed = (order[None, :] <= order[:, None]) & same_episode
    scores = jnp.einsum(
        "tkgd,skd->kgts",
        query.reshape(rows, local_kv, group, HEAD),
        key,
        preferred_element_type=jnp.float32,
    ) * (1.0 / HEAD**0.5)
    masked = jnp.where(allowed[None, None], scores, -1e30)
    largest = jnp.max(masked, -1, keepdims=True)
    expon = jnp.where(allowed[None, None], jnp.exp(masked - largest), 0.0)
    probs = (expon / jnp.sum(expon, -1, keepdims=True)).astype(jnp.bfloat16)
    output = jnp.einsum("kgts,skd->tkgd", probs, values_proj, preferred_element_type=jnp.float32)
    attended = output.astype(jnp.bfloat16).reshape(rows, local_heads * HEAD)
    all_heads = lax.all_gather(attended, "mp", axis=1, tiled=True)
    projected = jnp.dot(all_heads, whole_out, preferred_element_type=jnp.float32)
    feature_count = w_out.shape[1]
    own_states = lax.dynamic_slice_in_dim(
        states, lax.axis_index("mp") * feature_count, feature_count, 1
    )
    residual = own_states + projected
    square_sum, head_sum = lax.psum(
        (jnp.sum(residual * residual, 1), jnp.sum(residual * value_weight[None, :], 1)), "mp"
    )
    value = head_sum * lax.rsqrt(square_sum / width + epsilon)
    following = from_behind(old_values[:1], "dp", -1)
    next_old = jnp.concatenate([old_values[1:], following])
    booted = jnp.where(finished > 0, (1.0 - stopped) * old_values, next_old)
    delta = rewards + discount * booted - old_values
    keep_rate = discount * trace_decay
    spacing = (order[None, :] - order[:, None]).astype(jnp.float32)
    forward_mask = (spacing >= 0.0) & same_episode
    decay_matrix = jnp.where(
        forward_mask, jnp.power(jnp.float32(keep_rate), jnp.maximum(spacing, 0.0)), 0.0
    )
    local_part = jnp.dot(decay_matrix, delta, precision=lax.Precision.HIGHEST)
    remaining = (rows - order).astype(jnp.float32)
    reach = jnp.where(episode == episode[-1], jnp.power(jnp.float32(keep_rate), remaining), 0.0) * (
        1.0 - finished[-1]
    )

    def compose(earlier, later_map):
        return (later_map[0] + later_map[1] * earlier[0], later_map[1] * earlier[1])

    prefix = carried_in(
        (local_part[:1], reach[:1]),
        "dp",
        compose,
        (jnp.zeros((1,), jnp.float32), jnp.ones((1,), jnp.float32)),
    )
    incoming = prefix[0][0]
    advantage = local_part + reach * incoming
    returns = advantage + old_values
    clipped = old_values + jnp.clip(value - old_values, -clip_range, clip_range)
    terms = jnp.maximum((value - returns) ** 2, (clipped - returns) ** 2)
    total_loss = lax.psum(jnp.sum(terms), "dp")
    value_loss = 0.5 * total_loss / (rows * lax.axis_size("dp"))
    return (value, advantage, value_loss)


def solution(mesh):
    return jax.shard_map(
        body,
        mesh=mesh,
        in_specs=(
            P("dp", None),
            P("dp", "mp"),
            P("dp", "mp"),
            P("dp", "mp"),
            P("dp", "mp"),
            P("mp"),
            P("dp"),
            P("dp"),
            P(),
            P(),
        ),
        out_specs=(P("dp"), P("dp"), P()),
        check_vma=False,
    )
```

profile of v0, /device:TPU:0, one launch (start us, length us, event | category | flops | bytes accessed | tf_op | source)
XLA Modules:
  0.0 487.3 jit_solution(12846572343256018310)
XLA Ops:
  11.8 3.1 multiply_reduce_fusion
  15.1 1.0 multiply_cosine_fusion
  16.1 47.2 %all-gather.10.cloned.1.call-done = bf16[4096,512]{1,0:T(8,128)(2,1)} async-done(((bf16[256,512]{1,0:T(8,128)(2,1)}), bf16[4096,512]{1,0:T(8,128)(2,1)}) %all-gather.10.cloned.1.call-update) | async-done | bytes 4194320 | tf_op jit(solution)/shard_map/all_gather | solution.py:58
  63.3 5.9 %fusion.32 = f32[512,512]{0,1:T(8,128)S(1)} fusion(bf16[4096,512]{1,0:T(8,128)(2,1)} %all-gather.10.cloned.1.call-done, f32[512]{0:T(512)S(1)} %add_rsqrt_fusion, bf16[512,4096]{1,0:T(8,128)(2,1)} %param.12), kind=kOutput, calls=%fused_computation.70 | convolution fusion | flops 2153775104 | bytes 9439232 | tf_op jit(solution)/shard_map/dot_general | solution.py:64
  69.9 1.1 subtract_convert_fusion.1
  71.0 43.3 %all-gather.8.cloned.1.call-done = bf16[4096,512]{1,0:T(8,128)(2,1)} async-done(((bf16[256,512]{1,0:T(8,128)(2,1)}), bf16[4096,512]{1,0:T(8,128)(2,1)}) %all-gather.8.cloned.1.call-update) | async-done | bytes 4194320 | tf_op jit(solution)/shard_map/all_gather | solution.py:59
  114.4 5.9 %convolution_convert_fusion = bf16[512,512]{0,1:T(8,128)(2,1)S(1)} fusion(bf16[4096,512]{1,0:T(8,128)(2,1)} %all-gather.8.cloned.1.call-done, f32[512]{0:T(512)S(1)} %add_rsqrt_fusion, bf16[512,4096]{1,0:T(8,128)(2,1)} %param.12), kind=kOutput, calls=%fused_computation.26 | convolution fusion | flops 2154037248 | bytes 8914944 | tf_op jit(solution)/shard_map/dot_general | solution.py:64
  120.3 121.2 %all-gather.12.cloned.1.call-done = bf16[4096,2048]{1,0:T(8,128)(2,1)} async-done(((bf16[256,2048]{1,0:T(8,128)(2,1)}), bf16[4096,2048]{1,0:T(8,128)(2,1)}) %all-gather.12.cloned.1.call-update) | async-done | bytes 16777232 | tf_op jit(solution)/shard_map/all_gather | solution.py:57
  241.5 13.2 %convolution_bitcast_fusion = f32[64,8,16,128]{3,1,2,0:T(8,128)S(1)} fusion(bf16[4096,2048]{1,0:T(8,128)(2,1)} %all-gather.12.cloned.1.call-done, f32[512]{0:T(512)S(1)} %add_rsqrt_fusion, bf16[512,4096]{1,0:T(8,128)(2,1)} %param.12), kind=kOutput, calls=%fused_computation.18 | convolution fusion | flops 8596226048 | bytes 25167872 | tf_op jit(solution)/shard_map/dot_general | solution.py:64
  254.8 0.9 copy.36
  255.7 1.8 subtract_convert_fusion
  258.6 8.1 %fusion.6 = f32[4,512,512,4]{2,1,3,0:T(8,128)} fusion(bf16[512,4,4,64]{3,0,2,1:T(8,128)(2,1)S(1)} %bitcast.53, bf16[512,4,4,64]{3,0,2,1:T(8,128)(2,1)S(1)} %bitcast.54, bf16[512,4,64]{2,0,1:T(8,128)(2,1)S(1)} %copy-done, bf16[512,4,64]{2,0,1:T(8,128)(2,1)S(1)} %get-tuple-element.113), kind=kOutput, calls=%fused_computation.19 | convolution fusion | flops 1078984704 | bytes 19398656 | tf_op jit(solution)/shard_map/tkgd,skd->kgts/dot_general | solution.py:84
  266.8 17.9 %fusion.34 = (f32[4,4,512]{2,1,0:T(4,128)S(1)}, f32[4,4,512,512]{2,3,1,0:T(8,128)}) fusion(f32[4,512,512,4]{2,1,3,0:T(8,128)} %fusion.6, pred[512,512]{0,1:T(8,128)(4,1)S(1)} %compare_and_fusion.1), kind=kOutput, calls=%fused_computation.72 | output fusion | flops 29360640 | bytes 33849344 | tf_op jit(solution)/shard_map/sub | solution.py:92
  284.7 8.6 %fusion.10 = bf16[4,128,4,512]{3,1,2,0:T(8,128)(2,1)} fusion(bf16[512,4,128,1]{0,2,3,1:T(8,128)(2,1)S(1)} %bitcast.63, f32[4,4,512,512]{2,3,1,0:T(8,128)} %get-tuple-element.120, f32[4,4,512]{2,1,0:T(4,128)S(1)} %get-tuple-element.119), kind=kOutput, calls=%fused_computation.23 | convolution fusion | flops 1083179008 | bytes 19431424 | tf_op jit(solution)/shard_map/kgts,skd->tkgd/dot_general | solution.py:94
  293.9 1.3 collective-permute-start
  295.2 6.5 %convert_element_type.45 = f32[512,4096]{1,0:T(8,128)} convert(bf16[512,4096]{1,0:T(8,128)(2,1)} %param.12) | non-fusion elementwise | flops 2097152 | bytes 12582912 | tf_op jit(solution)/shard_map/convert_element_type | solution.py:52
  306.5 1.1 fusion.11
  308.3 34.8 %all-reduce.2 = (f32[16]{0:T(128)S(1)}, f32[16]{0:T(128)S(1)}) all-reduce(f32[16]{0:T(128)S(1)} %slice_dynamic-update-slice_fusion.1, f32[16]{0:T(128)S(1)} %slice_dynamic-update-slice_fusion), channel_id=2, replica_groups=mesh['dp'=16,'mp'=2] {'dp'}, use_global_device_ids=true, to_apply=%add | all-reduce | flops 32 | bytes 256
  343.1 28.6 %while.14 = (s32[]{:T(128)}, f32[1]{0:T(128)}, s32[]{:T(128)}, f32[16,1]{0,1:T(1,128)S(1)}, f32[16,1]{0,1:T(1,128)S(1)}, /*index=5*/s32[]{:T(128)}, s32[]{:T(128)}, s32[]{:T(128)}, s32[]{:T(128)}) while((s32[]{:T(128)}, f32[1]{0:T(128)}, s32[]{:T(128)}, f32[16,1]{0,1:T(1,128)S(1)}, f32[16,1]{0,1:T(1,128)S(1)}, /*index=5*/s32[]{:T(128)}, ...), condition=%wide.region_12.13_spmd, body=%wide.region_11.12_spmd.sunk | while | flops 8 | bytes 183 | solution.py:33
  371.7 53.4 %all-gather.14.cloned.1.call-done = bf16[512,4096]{0,1:T(8,128)(2,1)} async-done(((bf16[512,2048]{0,1:T(8,128)(2,1)}), bf16[512,4096]{0,1:T(8,128)(2,1)}) %all-gather.14.cloned.1.call-update) | async-done | bytes 4194320 | tf_op jit(solution)/shard_map/all_gather | solution.py:96
  425.1 14.6 %multiply_reduce_fusion.1 = (f32[512]{0:T(512)S(1)}, f32[512]{0:T(512)S(1)}) fusion(f32[2048]{0:T(1024)S(1)} %copy-done.3, bf16[512,4096]{0,1:T(8,128)(2,1)} %all-gather.14.cloned.1.call-done, bf16[4096,2048]{1,0:T(8,128)(2,1)} %all-gather.16.cloned.1.call-done, f32[512,4096]{1,0:T(8,128)} %convert_element_type.45, s32[]{:T(128)S(6)} %select_n.35), kind=kOutput, calls=%fused_computation.13 | convolution fusion | flops 8595177472 | bytes 25178116 | tf_op jit(solution)/shard_map/dot_general | solution.py:97
  439.7 4.9 %all-reduce.3 = (f32[512]{0:T(512)S(1)}, f32[512]{0:T(512)S(1)}) all-reduce(f32[512]{0:T(512)S(1)} %get-tuple-element.89, f32[512]{0:T(512)S(1)} %get-tuple-element.88), channel_id=1, replica_groups=mesh['dp'=16,'mp'=2] {'mp'}, use_global_device_ids=true, to_apply=%region_6.7 | all-reduce | flops 1024 | bytes 8192 | tf_op jit(solution)/shard_map/psum | solution.py:103
  444.7 1.9 maximum_reduce_fusion
  446.5 32.5 %psum.23 = f32[]{:T(128)} all-reduce(f32[]{:T(128)} %get-tuple-element.106), channel_id=1, replica_groups=mesh['dp'=16,'mp'=2] {'dp'}, use_global_device_ids=true, to_apply=%region_14.15 | all-reduce | flops 1 | bytes 8 | tf_op jit(solution)/shard_map/psum | solution.py:137
  (65 shorter events, 21.3 us)
Async XLA Ops:
  7.2 56.1 %all-gather.10.cloned.1.call-start = ((), (), s32[]{:S(2)}) async-start(), calls=%async_computation.1 | async-start | bytes 4456448 | tf_op jit(solution)/shard_map/all_gather | solution.py:58
  7.9 106.5 %all-gather.8.cloned.1.call-start = ((), (), s32[]{:S(2)}) async-start(), calls=%async_computation | async-start | bytes 4456448 | tf_op jit(solution)/shard_map/all_gather | solution.py:59
  8.7 232.9 %all-gather.12.cloned.1.call-start = ((), (), s32[]{:S(2)}) async-start(), calls=%async_computation.2 | async-start | bytes 17825792 | tf_op jit(solution)/shard_map/all_gather | solution.py:57
  9.4 362.3 %all-gather.16.cloned.1.call-start = ((), (), s32[]{:S(2)}) async-start(), calls=%async_computation.4 | async-start | bytes 17825792 | tf_op jit(solution)/shard_map/all_gather | solution.py:60
  10.0 415.2 %all-gather.14.cloned.1.call-start = ((), (), s32[]{:S(2)}) async-start(), calls=%async_computation.3 | async-start | bytes 6291456 | tf_op jit(solution)/shard_map/all_gather | solution.py:96
  257.5 1.1 copy-start
  284.7 8.6 %copy-start.1 = (f32[512]{0:T(512)S(1)}, f32[512]{0:T(512)}, u32[]{:S(2)}) copy-start(f32[512]{0:T(512)} %param.19) | copy-start | bytes 6148
  293.9 12.0 %collective-permute-start = (f32[1]{0:T(128)}, f32[1]{0:T(128)}, u32[]{:S(2)}, u32[]{:S(2)}) collective-permute-start(f32[1]{0:T(128)} %slice.35), channel_id=1, source_target_pairs={{2,0},{4,2},{6,4},{8,6},{10,8},{12,10},{14,12},{16,14},{18,16},{20... | collective-permute-start | bytes 20 | tf_op jit(solution)/shard_map/ppermute | solution.py:17
  295.2 8.6 %copy-start.4 = (u32[32]{0:T(128)S(1)}, u32[32]{0:T(128)}, u32[]{:S(2)}) copy-start(u32[32]{0:T(128)} %constant.106) | copy-start | bytes 388
  295.2 10.7 %copy-start.2 = (f32[512]{0:T(512)S(1)}, f32[512]{0:T(512)}, u32[]{:S(2)}) copy-start(f32[512]{0:T(512)} %param.18) | copy-start | bytes 6148
  295.2 130.0 %copy-start.3 = (f32[2048]{0:T(1024)S(1)}, f32[2048]{0:T(1024)}, u32[]{:S(2)}) copy-start(f32[2048]{0:T(1024)} %param.17) | copy-start | bytes 24580
Sparse Core Ops, SparseCore 0:
  10.1 53.0 all-gather.9
  65.4 48.8 all-gather.7
  116.5 124.9 all-gather.11
  243.6 125.2 all-gather.15
  370.2 54.8 all-gather.13
where the time goes:
time: 488 us; the launch traced here: 487 us
  waiting for transfers between devices  268 us (55%)
  blocking collectives  72.2 us (15%)
  matrix products  57.5 us (12%)
  other arithmetic  36 us (7%)
  loops' own time  19.3 us (4%)
  local copies, waits for them, and re-layouts  16.7 us (3%)
  between operations  16.4 us (3%)
    all_gather x1, waiting for transfers between devices, body(): lax.all_gather(w_query, 'dp', axis=0, tiled=True)  121 us
    all_gather x1, waiting for transfers between devices, body(): all_heads = lax.all_gather(attended, 'mp', axis=1, tiled=True)  53.4 us
    all_gather x1, waiting for transfers between devices, body(): lax.all_gather(w_key, 'dp', axis=0, tiled=True)  47.2 us
    all_gather x1, waiting for transfers between devices, body(): lax.all_gather(w_value, 'dp', axis=0, tiled=True)  43.3 us
    unnamed x1, blocking collectives  34.8 us
    psum x1, blocking collectives, body(): total_loss = lax.psum(jnp.sum(terms), 'dp')  32.5 us
    dot_general x3, matrix products, body(): jnp.dot(normed, piece, preferred_element_type=jnp.float32)  25 us
    another operation x1, loops' own time, carried_in(): return lax.fori_loop(0, ahead, one, state)  19.3 us
  transfers between devices with their start and end apart: 6, of which 4 were waited for; matrix products, arithmetic and copies ran while one was open for 19% of the time, Pallas kernels for 0%

commit v1 on v0

--- a/solution.py
+++ b/solution.py
@@ -93,7 +93,7 @@
     probs = (expon / jnp.sum(expon, -1, keepdims=True)).astype(jnp.bfloat16)
     output = jnp.einsum("kgts,skd->tkgd", probs, values_proj, preferred_element_type=jnp.float32)
     attended = output.astype(jnp.bfloat16).reshape(rows, local_heads * HEAD)
-    all_heads = lax.all_gather(attended, "mp", axis=1, tiled=True)
+    all_heads = jnp.concatenate(lax.all_gather(attended, "mp"), axis=1)
     projected = jnp.dot(all_heads, whole_out, preferred_element_type=jnp.float32)
     feature_count = w_out.shape[1]
     own_states = lax.dynamic_slice_in_dim(

time: 488 us -> 538 us (1.10)
  waiting for transfers between devices: 268 us -> 312 us
  local copies, waits for them, and re-layouts: 16.7 us -> 26.5 us
    all_gather x1, waiting for transfers between devices: 0.02 us -> 97.9 us  [body(): lax.all_gather(w_out, 'dp', axis=0, tiled=True)]
    all_gather x1, waiting for transfers between devices: 53.4 us -> 0.02 us  [body(): all_heads = jnp.concatenate(lax.all_gather(attended, 'mp'), axis=1)]
    all_gather x0 -> x1, local copies, waits for them, and re-layouts: none -> 6.28 us  [body(): all_heads = jnp.concatenate(lax.all_gather(attended, 'mp'), axis=1)]
  transfers between devices with their start and end apart: 6 -> 6, of which waited for: 4 -> 4; matrix products, arithmetic and copies ran while one was open for 19% -> 9% of each run, Pallas kernels for 0% -> 0%
where the time goes in v1:
time: 538 us; the launch traced here: 537 us
  waiting for transfers between devices  312 us (58%)
  blocking collectives  67.2 us (12%)
  matrix products  56.5 us (11%)
  other arithmetic  36.4 us (7%)
  local copies, waits for them, and re-layouts  26.5 us (5%)
  loops' own time  20.5 us (4%)
  between operations  16.5 us (3%)
    all_gather x1, waiting for transfers between devices, body(): lax.all_gather(w_query, 'dp', axis=0, tiled=True)  120 us
    all_gather x1, waiting for transfers between devices, body(): lax.all_gather(w_out, 'dp', axis=0, tiled=True)  97.9 us
    all_gather x1, waiting for transfers between devices, body(): lax.all_gather(w_key, 'dp', axis=0, tiled=True)  47.8 us
    all_gather x1, waiting for transfers between devices, body(): lax.all_gather(w_value, 'dp', axis=0, tiled=True)  43.3 us
    unnamed x1, blocking collectives  32.1 us
    psum x1, blocking collectives, body(): total_loss = lax.psum(jnp.sum(terms), 'dp')  30.2 us
    dot_general x3, matrix products, body(): jnp.dot(normed, piece, preferred_element_type=jnp.float32)  25.6 us
    another operation x1, loops' own time, carried_in(): return lax.fori_loop(0, ahead, one, state)  20.5 us
  transfers between devices with their start and end apart: 6, of which 4 were waited for; matrix products, arithmetic and copies ran while one was open for 9% of the time, Pallas kernels for 0%

profile of v1, /device:TPU:0, one launch (start us, length us, event | category | flops | bytes accessed | tf_op | source)
XLA Modules:
  0.0 537.2 jit_solution(15235032153322067136)
XLA Ops:
  11.2 3.1 multiply_reduce_fusion
  15.5 47.8 %all-gather.10.cloned.1.call-done = bf16[4096,512]{1,0:T(8,128)(2,1)} async-done(((bf16[256,512]{1,0:T(8,128)(2,1)}), bf16[4096,512]{1,0:T(8,128)(2,1)}) %all-gather.10.cloned.1.call-update) | async-done | bytes 4194320 | tf_op jit(solution)/shard_map/all_gather | solution.py:58
  63.3 5.9 %fusion.32 = f32[512,512]{0,1:T(8,128)S(1)} fusion(bf16[4096,512]{1,0:T(8,128)(2,1)} %all-gather.10.cloned.1.call-done, f32[512]{0:T(512)S(1)} %add_rsqrt_fusion, bf16[512,4096]{1,0:T(8,128)(2,1)} %param.12), kind=kOutput, calls=%fused_computation.70 | convolution fusion | flops 2153775104 | bytes 9439232 | tf_op jit(solution)/shard_map/dot_general | solution.py:64
  70.0 1.1 subtract_convert_fusion.1
  71.1 43.3 %all-gather.8.cloned.1.call-done = bf16[4096,512]{1,0:T(8,128)(2,1)} async-done(((bf16[256,512]{1,0:T(8,128)(2,1)}), bf16[4096,512]{1,0:T(8,128)(2,1)}) %all-gather.8.cloned.1.call-update) | async-done | bytes 4194320 | tf_op jit(solution)/shard_map/all_gather | solution.py:59
  114.4 6.7 %convolution_convert_fusion = bf16[512,512]{0,1:T(8,128)(2,1)} fusion(bf16[4096,512]{1,0:T(8,128)(2,1)} %all-gather.8.cloned.1.call-done, f32[512]{0:T(512)S(1)} %add_rsqrt_fusion, bf16[512,4096]{1,0:T(8,128)(2,1)} %param.12), kind=kOutput, calls=%fused_computation.26 | convolution fusion | flops 2154037248 | bytes 8914944 | tf_op jit(solution)/shard_map/dot_general | solution.py:64
  121.1 120.4 %all-gather.12.cloned.1.call-done = bf16[4096,2048]{1,0:T(8,128)(2,1)} async-done(((bf16[256,2048]{1,0:T(8,128)(2,1)}), bf16[4096,2048]{1,0:T(8,128)(2,1)}) %all-gather.12.cloned.1.call-update) | async-done | bytes 16777232 | tf_op jit(solution)/shard_map/all_gather | solution.py:57
  241.5 13.0 %convolution_bitcast_fusion = f32[64,8,16,128]{3,1,2,0:T(8,128)S(1)} fusion(bf16[4096,2048]{1,0:T(8,128)(2,1)} %all-gather.12.cloned.1.call-done, f32[512]{0:T(512)S(1)} %add_rsqrt_fusion, bf16[512,4096]{1,0:T(8,128)(2,1)} %param.12), kind=kOutput, calls=%fused_computation.18 | convolution fusion | flops 8596226048 | bytes 25167872 | tf_op jit(solution)/shard_map/dot_general | solution.py:64
  255.5 1.6 subtract_convert_fusion
  258.2 8.2 %fusion.6 = f32[4,512,512,4]{2,1,3,0:T(8,128)} fusion(bf16[512,4,4,64]{3,0,2,1:T(8,128)(2,1)S(1)} %bitcast.56, bf16[512,4,4,64]{3,0,2,1:T(8,128)(2,1)S(1)} %bitcast.57, bf16[512,4,64]{2,0,1:T(8,128)(2,1)S(1)} %copy-done, bf16[512,4,64]{2,0,1:T(8,128)(2,1)S(1)} %get-tuple-element.113), kind=kOutput, calls=%fused_computation.19 | convolution fusion | flops 1078984704 | bytes 19398656 | tf_op jit(solution)/shard_map/tkgd,skd->kgts/dot_general | solution.py:84
  266.3 17.8 %fusion.34 = (f32[4,4,512]{2,1,0:T(4,128)S(1)}, f32[4,4,512,512]{2,3,1,0:T(8,128)}) fusion(f32[4,512,512,4]{2,1,3,0:T(8,128)} %fusion.6, pred[512,512]{0,1:T(8,128)(4,1)S(1)} %compare_and_fusion.1), kind=kOutput, calls=%fused_computation.72 | output fusion | flops 29360640 | bytes 33849344 | tf_op jit(solution)/shard_map/sub | solution.py:92
  284.2 7.1 %fusion.10 = bf16[4,128,4,512]{3,1,2,0:T(8,128)(2,1)S(1)} fusion(bf16[512,4,128,1]{0,2,3,1:T(8,128)(2,1)S(1)} %bitcast.67, f32[4,4,512,512]{2,3,1,0:T(8,128)} %get-tuple-element.120, f32[4,4,512]{2,1,0:T(4,128)S(1)} %get-tuple-element.119), kind=kOutput, calls=%fused_computation.23 | convolution fusion | flops 1083179008 | bytes 19431424 | tf_op jit(solution)/shard_map/kgts,skd->tkgd/dot_general | solution.py:94
  291.2 2.5 copy.46
  294.9 1.3 collective-permute-start
  296.2 7.3 %convert_element_type.45 = f32[512,4096]{1,0:T(8,128)} convert(bf16[512,4096]{1,0:T(8,128)(2,1)} %param.12) | non-fusion elementwise | flops 2097152 | bytes 12582912 | tf_op jit(solution)/shard_map/convert_element_type | solution.py:52
  308.5 1.1 fusion.11
  310.4 32.1 %all-reduce.2 = (f32[16]{0:T(128)S(1)}, f32[16]{0:T(128)S(1)}) all-reduce(f32[16]{0:T(128)S(1)} %slice_dynamic-update-slice_fusion.1, f32[16]{0:T(128)S(1)} %slice_dynamic-update-slice_fusion), channel_id=2, replica_groups=mesh['dp'=16,'mp'=2] {'dp'}, use_global_device_ids=true, to_apply=%add | all-reduce | flops 32 | bytes 256
  342.5 30.6 %while.14 = (s32[]{:T(128)}, f32[1]{0:T(128)}, s32[]{:T(128)}, f32[16,1]{0,1:T(1,128)S(1)}, f32[16,1]{0,1:T(1,128)S(1)}, /*index=5*/s32[]{:T(128)}, s32[]{:T(128)}, s32[]{:T(128)}, s32[]{:T(128)}) while((s32[]{:T(128)}, f32[1]{0:T(128)}, s32[]{:T(128)}, f32[16,1]{0,1:T(1,128)S(1)}, f32[16,1]{0,1:T(1,128)S(1)}, /*index=5*/s32[]{:T(128)}, ...), condition=%wide.region_12.13_spmd, body=%wide.region_11.12_spmd.sunk | while | flops 8 | bytes 183 | solution.py:33
  373.1 6.3 %copy.47 = bf16[2,512,2048]{1,2,0:T(8,128)(2,1)} copy(bf16[2,512,2048]{2,1,0:T(8,128)(2,1)} %all-gather.14.cloned.1.call-done) | data formatting | bytes 8388608 | tf_op jit(solution)/shard_map/all_gather | solution.py:96
  379.4 97.9 %all-gather.16.cloned.1.call-done = bf16[4096,2048]{1,0:T(8,128)(2,1)} async-done(((bf16[256,2048]{1,0:T(8,128)(2,1)}), bf16[4096,2048]{1,0:T(8,128)(2,1)}) %all-gather.16.cloned.1.call-update) | async-done | bytes 16777232 | tf_op jit(solution)/shard_map/all_gather | solution.py:60
  477.3 14.6 %multiply_reduce_fusion.1 = (f32[512]{0:T(512)S(1)}, f32[512]{0:T(512)S(1)}) fusion(f32[2048]{0:T(1024)S(1)} %copy-done.3, bf16[512,4096]{0,1:T(8,128)(2,1)} %bitcast.58, bf16[4096,2048]{1,0:T(8,128)(2,1)} %all-gather.16.cloned.1.call-done, f32[512,4096]{1,0:T(8,128)} %convert_element_type.45, s32[]{:T(128)S(6)} %select_n.35), kind=kOutput, calls=%fused_computation.13 | convolution fusion | flops 8595177472 | bytes 25178116 | tf_op jit(solution)/shard_map/dot_general | solution.py:97
  491.9 4.9 all-reduce.3
  496.9 1.9 maximum_reduce_fusion
  498.7 30.2 %psum.23 = f32[]{:T(128)} all-reduce(f32[]{:T(128)} %get-tuple-element.106), channel_id=1, replica_groups=mesh['dp'=16,'mp'=2] {'dp'}, use_global_device_ids=true, to_apply=%region_14.15 | all-reduce | flops 1 | bytes 8 | tf_op jit(solution)/shard_map/psum | solution.py:137
  (69 shorter events, 24.2 us)
Async XLA Ops:
  7.2 56.1 %all-gather.10.cloned.1.call-start = ((), (), s32[]{:S(2)}) async-start(), calls=%async_computation.1 | async-start | bytes 4456448 | tf_op jit(solution)/shard_map/all_gather | solution.py:58
  7.9 106.5 %all-gather.8.cloned.1.call-start = ((), (), s32[]{:S(2)}) async-start(), calls=%async_computation | async-start | bytes 4456448 | tf_op jit(solution)/shard_map/all_gather | solution.py:59
  8.7 232.9 %all-gather.12.cloned.1.call-start = ((), (), s32[]{:S(2)}) async-start(), calls=%async_computation.2 | async-start | bytes 17825792 | tf_op jit(solution)/shard_map/all_gather | solution.py:57
  9.4 363.7 %all-gather.14.cloned.1.call-start = ((), (), s32[]{:S(2)}) async-start(), calls=%async_computation.3 | async-start | bytes 6291456 | tf_op jit(solution)/shard_map/all_gather | solution.py:96
  257.1 1.1 copy-start
  266.3 17.8 %copy-start.4 = (bf16[512,512]{0,1:T(8,128)(2,1)S(1)}, bf16[512,512]{0,1:T(8,128)(2,1)}, u32[]{:S(2)}) copy-start(bf16[512,512]{0,1:T(8,128)(2,1)} %convolution_convert_fusion) | copy-start | bytes 1572868
  291.2 3.2 copy-start.1
  293.8 183.5 %all-gather.16.cloned.1.call-start = ((), (), s32[]{:S(2)}) async-start(), calls=%async_computation.4 | async-start | bytes 17825792 | tf_op jit(solution)/shard_map/all_gather | solution.py:60
  294.9 12.8 %collective-permute-start = (f32[1]{0:T(128)}, f32[1]{0:T(128)}, u32[]{:S(2)}, u32[]{:S(2)}) collective-permute-start(f32[1]{0:T(128)} %slice.35), channel_id=1, source_target_pairs={{2,0},{4,2},{6,4},{8,6},{10,8},{12,10},{14,12},{16,14},{18,16},{20... | collective-permute-start | bytes 20 | tf_op jit(solution)/shard_map/ppermute | solution.py:17
  296.2 9.5 %copy-start.5 = (u32[32]{0:T(128)S(1)}, u32[32]{0:T(128)}, u32[]{:S(2)}) copy-start(u32[32]{0:T(128)} %constant.106) | copy-start | bytes 388
  296.2 11.5 %copy-start.2 = (f32[512]{0:T(512)S(1)}, f32[512]{0:T(512)}, u32[]{:S(2)}) copy-start(f32[512]{0:T(512)} %param.18) | copy-start | bytes 6148
  373.1 104.2 %copy-start.3 = (f32[2048]{0:T(1024)S(1)}, f32[2048]{0:T(1024)}, u32[]{:S(2)}) copy-start(f32[2048]{0:T(1024)} %param.17) | copy-start | bytes 24580
Sparse Core Ops, SparseCore 0:
  10.1 53.0 all-gather.9
  65.4 48.8 all-gather.7
  116.5 124.9 all-gather.11
  293.9 54.8 all-gather.13
  350.8 126.4 all-gather.15
